TPU v7x, 256 devices: a whole 4x4x8 slice. The times are simulated.
256 devices in a mesh: bead: 16 (over x, z_lo), slab: 8 (over y, z_hi), grp: 2 (over core).
Axes of the slice: x: 4, y: 4, z: 8 (z_hi: 2, z_lo: 4; z = z_hi * 4 + z_lo), core: 2. Of those that a mesh axis runs over, the one named last changes fastest.
Arguments:
- positions: float32 [64, 3, 65536], P('bead', None, ('slab', 'grp')), may hold values from -6 to 6
- momenta: float32 [64, 3, 65536], P('bead', None, ('slab', 'grp')), may hold values from -12 to 12
- force_old: float32 [64, 3, 65536], P('bead', None, ('slab', 'grp')), may hold values from -6 to 6
- noise: float32 [64, 3, 65536], P('bead', None, ('slab', 'grp')), may hold values from -6 to 6
- mass: float32 [65536], P(('slab', 'grp')), may hold values from 1 to 16
- pair_list: int32 [65536, 32], P(('slab', 'grp')), may hold values from 0 to 4351, as said below
- desc_w: bfloat16 [128, 1600], replicated, may hold values from -0.5 to 0.5
- hidden_one: bfloat16 [1600, 240], replicated, may hold values from -0.15625 to 0.15625
- hidden_two: bfloat16 [240, 240], replicated, may hold values from -0.375 to 0.375
- hidden_three: bfloat16 [240, 240], replicated, may hold values from -0.375 to 0.375
- out_w: bfloat16 [240, 3], replicated, may hold values from -0.375 to 0.375
Outputs:
- new_positions: float32 [64, 3, 65536], P('bead', None, ('slab', 'grp'))
- new_momenta: float32 [64, 3, 65536], P('bead', None, ('slab', 'grp'))
- force_new: float32 [64, 3, 65536], P('bead', None, ('slab', 'grp'))
Inputs may be any that keep to these rules, and one draw needn't show every extreme that they name: `pair_list`: for the atom with index li in its slab, every entry lies in li .. li + 256; entries past a count of 16 to 32 per atom name the atom itself, li + 128.
All inputs are finite; a program needn't handle non-finite values.
Results may differ from a plain program's by a relative error of at most 0.00096.
Values sent between devices are 32-bit elements; how exact they have to be, the bound alone decides.
A program may use at most 128 MiB of HBM per device.

v0:
```python
import math
import jax
import jax.numpy as jnp
from jax import lax
from jax.sharding import PartitionSpec as P

BEADS = 64
NC = 8
EDGE = 128
TIME_STEP = 0.1
CYCLE_FREQ = 5.0
CENTROID_FRICTION = 1.0
PAIR_STRENGTH = 0.5


def padded(shard, sides, width):
    for axis, dim in sides:
        count, length = (lax.axis_size(axis), shard.shape[dim])
        up = [(i, (i + 1) % count) for i in range(count)]
        down = [(j, i) for i, j in up]
        last = lax.slice_in_dim(shard, length - width, length, axis=dim)
        first = lax.slice_in_dim(shard, 0, width, axis=dim)
        before = lax.ppermute(last, axis, up)
        after = lax.ppermute(first, axis, down)
        shard = jnp.concatenate([before, shard, after], axis=dim)
    return shard


def cycle_tables(beads, contracted):
    index = jnp.arange(beads, dtype=jnp.float32)
    mode_int = jnp.arange(beads, dtype=jnp.int32)[None, :]
    angle = 2.0 * jnp.pi * index[:, None] * index[None, :] / beads
    half_mode = beads // 2
    root_one = 1.0 / jnp.sqrt(jnp.float32(beads))
    root_two = jnp.sqrt(2.0 / jnp.float32(beads))
    basis = jnp.where(
        mode_int == 0,
        root_one * jnp.ones_like(angle),
        jnp.where(
            mode_int < half_mode,
            root_two * jnp.cos(angle),
            jnp.where(mode_int == half_mode, root_one * jnp.cos(angle), root_two * jnp.sin(angle)),
        ),
    )
    freq = 2.0 * CYCLE_FREQ * jnp.sin(jnp.pi * index / beads)
    cindex = jnp.arange(contracted, dtype=jnp.float32)
    spacing = index[None, :] / beads - cindex[:, None] / contracted
    kernel = jnp.ones_like(spacing)
    for order in range(1, contracted // 2):
        kernel = kernel + 2.0 * jnp.cos(2.0 * jnp.pi * order * spacing)
    kernel = kernel + jnp.cos(jnp.pi * contracted * spacing)
    return (basis, freq, kernel / beads)


def free_drift(modes_q, modes_p, freq, masses):
    step = 0.5 * TIME_STEP
    rate = freq[:, None, None]
    moving = rate > 0.0
    safe = jnp.where(moving, rate, 1.0)
    cosine = jnp.cos(safe * step)
    sine = jnp.sin(safe * step)
    new_q = jnp.where(
        moving,
        cosine * modes_q + sine / (masses * safe) * modes_p,
        modes_q + step * modes_p / masses,
    )
    new_p = jnp.where(moving, cosine * modes_p - masses * safe * sine * modes_q, modes_p)
    return (new_q, new_p)


def thermostat(modes_p, noise, freq, masses):
    friction = jnp.where(freq > 0.0, 2.0 * freq, CENTROID_FRICTION)
    keep = jnp.exp(-friction * TIME_STEP)[:, None, None]
    return keep * modes_p + jnp.sqrt(masses) * jnp.sqrt(1.0 - keep * keep) * noise


def banded_take(extended, lists, start):
    copies = extended.shape[0]
    count, width = lists.shape
    block = math.gcd(count, 128)
    span = block + 2 * EDGE
    flat = extended.reshape(copies * 3, extended.shape[2])
    columns = jnp.arange(span, dtype=jnp.int32)[:, None]

    def one_block(number):
        first = start + number * block
        window = lax.dynamic_slice_in_dim(flat, first, span, 1)
        rows = lax.dynamic_slice_in_dim(lists, number * block, block, 0) - first
        selector = (rows.reshape(1, block * width) == columns).astype(jnp.float32)
        picked = jnp.dot(
            window, selector, precision=lax.Precision.HIGHEST, preferred_element_type=jnp.float32
        )
        return picked.reshape(copies, 3, block, width)

    pieces = lax.map(one_block, jnp.arange(count // block, dtype=jnp.int32))
    return jnp.transpose(pieces, (1, 2, 0, 3, 4)).reshape(copies, 3, count, width)


def contracted_forces(extended, lists, start, weights):
    desc_w, hidden_one, hidden_two, hidden_three, out_w = weights
    count = lists.shape[0]
    copies = extended.shape[0]
    near = banded_take(extended, lists, start)
    own = lax.dynamic_slice_in_dim(extended, start + EDGE, count, 2)[:, :, :, None]
    apart = near - own
    closeness = 1.0 / (1.0 + jnp.sum(apart * apart, axis=1))
    env = jnp.concatenate([apart, closeness[:, None]], axis=1)
    env = jnp.transpose(env, (0, 2, 3, 1)).reshape(copies * count, -1).astype(jnp.bfloat16)
    layer = jnp.tanh(jnp.dot(env, desc_w, preferred_element_type=jnp.float32)).astype(jnp.bfloat16)
    for matrix in (hidden_one, hidden_two, hidden_three):
        layer = jnp.tanh(jnp.dot(layer, matrix, preferred_element_type=jnp.float32)).astype(
            jnp.bfloat16
        )
    output = jnp.dot(layer, out_w, preferred_element_type=jnp.float32)
    return jnp.transpose(output.reshape(copies, count, 3), (0, 2, 1))


def pair_forces(extended, lists):
    count = lists.shape[0]
    near = banded_take(extended, lists, jnp.int32(0))
    own = extended[:, :, EDGE : EDGE + count][:, :, :, None]
    apart = near - own
    closeness = 1.0 / (1.0 + jnp.sum(apart * apart, axis=1, keepdims=True))
    return PAIR_STRENGTH * jnp.sum(apart * closeness, axis=3)


def slab_edges(field):
    return padded(field, ((("slab", "grp"), 2),), EDGE)


def body(
    positions,
    momenta,
    force_old,
    noise,
    mass,
    pair_list,
    desc_w,
    hidden_one,
    hidden_two,
    hidden_three,
    out_w,
):
    best = lax.Precision.HIGHEST
    beads_local = positions.shape[0]
    slab_atoms = positions.shape[2]
    groups = lax.axis_size("bead")
    block_rows = slab_atoms // groups
    place = lax.axis_index("bead")
    start = place * block_rows
    basis, freq, contract = cycle_tables(BEADS, NC)
    weights = (desc_w, hidden_one, hidden_two, hidden_three, out_w)
    ratio = BEADS / NC
    kicked = momenta + 0.5 * TIME_STEP * force_old
    gathered_q, gathered_p, mode_noise = (
        lax.all_to_all(positions, "bead", split_axis=2, concat_axis=0, tiled=True),
        lax.all_to_all(kicked, "bead", split_axis=2, concat_axis=0, tiled=True),
        lax.all_to_all(noise, "bead", split_axis=2, concat_axis=0, tiled=True),
    )
    masses = lax.dynamic_slice_in_dim(mass, start, block_rows, 0)[None, None, :]
    modes_q = jnp.einsum("bk,bxa->kxa", basis, gathered_q, precision=best)
    modes_p = jnp.einsum("bk,bxa->kxa", basis, gathered_p, precision=best)
    modes_q, modes_p = free_drift(modes_q, modes_p, freq, masses)
    modes_p = thermostat(modes_p, mode_noise, freq, masses)
    modes_q, modes_p = free_drift(modes_q, modes_p, freq, masses)
    block_q = jnp.einsum("bk,kxa->bxa", basis, modes_q, precision=best)
    block_p = jnp.einsum("bk,kxa->bxa", basis, modes_p, precision=best)
    row_lists = lax.dynamic_slice_in_dim(pair_list, start, block_rows, 0)
    local_contract = lax.dynamic_slice_in_dim(contract, place * beads_local, beads_local, 1)
    new_q, moved = (
        lax.all_to_all(block_q, "bead", split_axis=0, concat_axis=2, tiled=True),
        lax.all_to_all(block_p, "bead", split_axis=0, concat_axis=2, tiled=True),
    )
    bead_terms = jnp.einsum("cb,bxa->cxa", local_contract, new_q, precision=best)
    slab_contracted = lax.psum(bead_terms, "bead")
    neural = contracted_forces(slab_edges(slab_contracted), row_lists, start, weights)
    spread = ratio * jnp.einsum(
        "cb,cxa->bxa",
        local_contract,
        lax.all_gather(neural, "bead", axis=2, tiled=True),
        precision=best,
    )
    bead_extended = padded(new_q, ((("slab", "grp"), 2),), EDGE)
    pairs = pair_forces(bead_extended, pair_list)
    force_new = pairs + spread
    return (new_q, moved + 0.5 * TIME_STEP * force_new, force_new)


def solution(mesh):
    placed = (
        P("bead", None, ("slab", "grp")),
        P("bead", None, ("slab", "grp")),
        P("bead", None, ("slab", "grp")),
        P("bead", None, ("slab", "grp")),
        P(("slab", "grp")),
        P(("slab", "grp"), None),
        P(),
        P(),
        P(),
        P(),
        P(),
    )
    return jax.shard_map(
        body,
        mesh=mesh,
        in_specs=placed,
        out_specs=(
            P("bead", None, ("slab", "grp")),
            P("bead", None, ("slab", "grp")),
            P("bead", None, ("slab", "grp")),
        ),
        check_vma=False,
    )
```

profile of v0, /device:TPU:0, one launch (start us, length us, event | category | flops | bytes accessed | tf_op | source)
XLA Modules:
  0.0 457.1 jit_solution(15007762217400926848)
XLA Ops:
  7.2 6.7 %copy.125 = f32[4,3,4096]{0,1,2:T(4,128)} copy(f32[4,3,4096]{2,0,1:T(4,128)} %param.18) | data formatting | bytes 393216 | tf_op args[3]
  13.9 8.9 %reshape.263 = f32[16,1,3072]{2,1,0:T(1,128)} reshape(f32[4096,3,4]{2,1,0:T(4,128)} %bitcast.121) | data formatting | bytes 393216
  22.8 6.8 %all-to-all-start.2 = ((f32[16,1,3072]{2,1,0:T(1,128)}), f32[16,1,3072]{2,1,0:T(1,128)S(1)}, u32[]{:S(2)}, u32[]{:S(2)}) async-start(f32[16,1,3072]{2,1,0:T(1,128)} %reshape.263), calls=%async_computation.2 | async-start | bytes 393216 | tf_op jit(solution)/shard_map/all_to_all | solution.py:158
  29.8 6.0 %copy.119 = f32[4,3,4096]{0,1,2:T(4,128)} copy(f32[4,3,4096]{2,0,1:T(4,128)S(1)} %copy-done.5) | data formatting | bytes 393216 | tf_op args[0]
  35.7 8.9 %reshape.267 = f32[16,1,3072]{2,1,0:T(1,128)} reshape(f32[4096,3,4]{2,1,0:T(4,128)} %bitcast.122) | data formatting | bytes 393216
  44.9 7.5 %all-to-all-start = ((f32[16,1,3072]{2,1,0:T(1,128)}), f32[16,1,3072]{2,1,0:T(1,128)S(1)}, u32[]{:S(2)}, u32[]{:S(2)}) async-start(f32[16,1,3072]{2,1,0:T(1,128)} %reshape.267), calls=%async_computation | async-start | bytes 393216 | tf_op jit(solution)/shard_map/all_to_all | solution.py:156
  52.5 6.0 %copy.122 = f32[4,3,4096]{0,1,2:T(4,128)} copy(f32[4,3,4096]{2,0,1:T(4,128)S(1)} %multiply_add_fusion.2) | data formatting | bytes 393216 | tf_op jit(solution)/shard_map/add | solution.py:154
  58.4 8.9 %reshape.265 = f32[16,1,3072]{2,1,0:T(1,128)} reshape(f32[4096,3,4]{2,1,0:T(4,128)} %bitcast.117) | data formatting | bytes 393216
  67.5 8.0 %all-to-all-start.1 = ((f32[16,1,3072]{2,1,0:T(1,128)}), f32[16,1,3072]{2,1,0:T(1,128)S(1)}, u32[]{:S(2)}, u32[]{:S(2)}) async-start(f32[16,1,3072]{2,1,0:T(1,128)} %reshape.265), calls=%async_computation.1 | async-start | bytes 393216 | tf_op jit(solution)/shard_map/all_to_all | solution.py:157
  78.0 7.2 %reshape.264 = f32[4096,3,4]{2,1,0:T(4,128)} reshape(f32[16,3072]{1,0:T(8,128)S(1)} %reduce.3) | data formatting | bytes 393216
  85.2 6.5 %copy.126 = f32[4,3,16,256]{3,0,2,1:T(4,128)S(1)} copy(f32[4,3,16,256]{0,1,3,2:T(4,128)} %bitcast.118) | data formatting | bytes 393216 | tf_op jit(solution)/shard_map/all_to_all | solution.py:158
  92.9 7.2 %reshape.268 = f32[4096,3,4]{2,1,0:T(4,128)} reshape(f32[16,3072]{1,0:T(8,128)S(1)} %reduce.4) | data formatting | bytes 393216
  100.1 6.5 %copy.120 = f32[4,3,16,256]{3,0,2,1:T(4,128)S(1)} copy(f32[4,3,16,256]{0,1,3,2:T(4,128)} %bitcast.119) | data formatting | bytes 393216 | tf_op jit(solution)/shard_map/all_to_all | solution.py:156
  107.8 7.2 %reshape.266 = f32[4096,3,4]{2,1,0:T(4,128)} reshape(f32[16,3072]{1,0:T(8,128)S(1)} %reduce.5) | data formatting | bytes 393216
  115.0 6.6 %copy.123 = f32[4,3,16,256]{3,0,2,1:T(4,128)S(1)} copy(f32[4,3,16,256]{0,1,3,2:T(4,128)} %bitcast.120) | data formatting | bytes 393216 | tf_op jit(solution)/shard_map/all_to_all | solution.py:157
  124.3 7.6 %all-to-all-start.3 = ((f32[64,3,256]{2,1,0:T(4,128)}), f32[64,3,256]{2,1,0:T(4,128)S(1)}, u32[]{:S(2)}, u32[]{:S(2)}) async-start(f32[64,3,256]{2,1,0:T(4,128)} %copy.127), calls=%async_computation.3 | async-start | bytes 524288 | tf_op jit(solution)/shard_map/all_to_all | solution.py:171
  136.4 4.6 %all-to-all-done.3 = f32[64,3,256]{2,1,0:T(4,128)S(1)} async-done(((f32[64,3,256]{2,1,0:T(4,128)}), f32[64,3,256]{2,1,0:T(4,128)S(1)}, u32[]{:S(2)}, u32[]{:S(2)}) %all-to-all-start.3) | async-done | bytes 196640 | tf_op jit(solution)/shard_map/all_to_all | solution.py:171
  141.0 3.7 all-to-all-start.4
  145.0 3.4 collective-permute-start.1
  149.9 3.9 all-to-all-done.4
  154.5 3.0 collective-permute-done
  157.6 173.7 %while.22 = (s32[]{:T(128)}, f32[32,4,3,128,32]{4,3,2,1,0:T(8,128)}, s32[32]{0:T(128)S(1)}, f32[12,4352]{1,0:T(8,128)S(1)}, s32[4096,32]{1,0:T(8,128)}, /*index=...) while((s32[]{:T(128)}, f32[32,4,3,128,32]{4,3,2,1,0:T(8,128)}, s32[32]{0:T(128)S(1)}, ...), condition=%wide.region_1.2_spmd.clone, body=%wide.region_0.1_spmd.clone.sunk | while | flops 228069376 | bytes 1679568 | solution.py:95
  159.8 2.0 fusion.127
  165.2 2.0 fusion.127
  170.6 2.0 fusion.127
  176.1 2.0 fusion.127
  181.5 2.0 fusion.127
  186.9 2.0 fusion.127
  192.3 2.0 fusion.127
  241.2 2.0 fusion.127
  252.0 2.0 fusion.127
  279.2 2.0 fusion.127
  290.0 2.0 fusion.127
  295.4 2.0 fusion.127
  300.8 2.0 fusion.127
  306.2 2.0 fusion.127
  322.5 2.0 fusion.127
  331.2 14.3 %multiply_reduce_fusion.1 = f32[4,32,128,32]{3,2,0,1:T(8,128)} fusion(f32[32,4,3,128,32]{4,3,2,1,0:T(8,128)} %get-tuple-element.72, f32[4,3,32,128]{3,1,0,2:T(4,128)S(1)} %copy.135), kind=kLoop, calls=%fused_computation.18 | loop fusion | flops 4194304 | bytes 8585216 | tf_op jit(solution)/shard_map/reduce_sum | solution.py:123
  345.5 4.5 add_divide_fusion
  350.0 16.5 %multiply_reduce_fusion = f32[4,3,32,128]{3,1,0,2:T(4,128)S(1)} fusion(f32[32,4,3,128,32]{4,3,2,1,0:T(8,128)} %get-tuple-element.72, f32[4,32,128,32]{3,2,0,1:T(8,128)S(1)} %add_divide_fusion, f32[4,3,32,128]{3,1,0,2:T(4,128)S(1)} %copy.135), kind=kLoop, calls=%fused_computation.17 | loop fusion | flops 4669440 | bytes 8781824 | tf_op jit(solution)/shard_map/reduce_sum | solution.py:124
  367.4 8.0 %collective-permute-start.3 = (f32[8,3,128]{2,0,1:T(8,128)S(1)}, f32[8,3,128]{2,0,1:T(8,128)S(1)}, u32[]{:S(2)}, u32[]{:S(2)}) collective-permute-start(f32[8,3,128]{2,0,1:T(8,128)S(1)} %get-tuple-element.149), channel_id=1, source_target_pairs={{1,0},{2,1},{3,2},{4,3},{5,4},{6,5},{7,6},{8,7},{9,8},{10,9},{11,1... | collective-permute-start | bytes 36872 | tf_op jit(solution)/shard_map/ppermute | solution.py:24
  378.7 11.8 %while.23 = (s32[]{:T(128)}, f32[2,8,3,128,32]{4,3,2,1,0:T(8,128)}, s32[2]{0:T(128)S(1)}, s32[]{:T(128)}, f32[24,4352]{1,0:T(8,128)}, /*index=5*/s32[256,32]{1,0...) while((s32[]{:T(128)}, f32[2,8,3,128,32]{4,3,2,1,0:T(8,128)}, ...), condition=%wide.region_6.7_spmd.clone, body=%wide.region_5.6_spmd.clone.sunk | while | flops 454561792 | bytes 3264749 | solution.py:95
  380.1 2.8 fusion.129
  386.0 2.8 fusion.129
  390.6 2.5 multiply_reduce_fusion.2
  393.6 2.4 copy.141
  397.3 4.6 %fusion.15 = bf16[2048,240]{0,1:T(8,128)(2,1)S(1)} fusion(bf16[1600,240]{0,1:T(8,128)(2,1)S(1)} %copy-done, bf16[128,1600]{0,1:T(8,128)(2,1)} %param.21, bf16[2048,128]{0,1:T(8,128)(2,1)S(1)} %bitcast.138), kind=kOutput, calls=%fused_computation.28 | convolution fusion | flops 2415493120 | bytes 2684928 | tf_op jit(solution)/shard_map/dot_general | solution.py:111
  403.0 45.6 %all_gather.3 = f32[8,3,4096]{2,0,1:T(8,128)S(1)} all-gather(f32[8,3,256]{2,0,1:T(8,128)S(1)} %bitcast.140), channel_id=1, replica_groups=mesh['bead'=16,'slab'=8,'grp'=2] {'bead'}, dimensions={2}, use_global_device_ids=true | all-gather | bytes 417792 | tf_op jit(solution)/shard_map/all_gather | solution.py:180
  (291 shorter events, 150.8 us)
Async XLA Ops:
  7.2 390.1 %copy-start = (bf16[1600,240]{0,1:T(8,128)(2,1)S(1)}, bf16[1600,240]{0,1:T(8,128)(2,1)}, u32[]{:S(2)}) copy-start(bf16[1600,240]{0,1:T(8,128)(2,1)} %param.22) | copy-start | bytes 2304004
  7.2 22.4 %copy-start.3 = (f32[4,3,4096]{2,0,1:T(4,128)S(1)}, f32[4,3,4096]{2,0,1:T(4,128)}, u32[]{:S(2)}) copy-start(f32[4,3,4096]{2,0,1:T(4,128)} %param.16) | copy-start | bytes 589828
  7.2 22.4 %copy-start.4 = (f32[4,3,4096]{2,0,1:T(4,128)S(1)}, f32[4,3,4096]{2,0,1:T(4,128)}, u32[]{:S(2)}) copy-start(f32[4,3,4096]{2,0,1:T(4,128)} %param.17) | copy-start | bytes 589828
  7.2 22.6 %copy-start.5 = (f32[4,3,4096]{2,0,1:T(4,128)S(1)}, f32[4,3,4096]{2,0,1:T(4,128)}, u32[]{:S(2)}) copy-start(f32[4,3,4096]{2,0,1:T(4,128)} %param.15) | copy-start | bytes 589828
  22.8 22.1 %all-to-all-start.2 = ((f32[16,1,3072]{2,1,0:T(1,128)}), f32[16,1,3072]{2,1,0:T(1,128)S(1)}, u32[]{:S(2)}, u32[]{:S(2)}) async-start(f32[16,1,3072]{2,1,0:T(1,128)} %reshape.263), calls=%async_computation.2 | async-start | bytes 393216 | tf_op jit(solution)/shard_map/all_to_all | solution.py:158
  44.9 22.5 %all-to-all-start = ((f32[16,1,3072]{2,1,0:T(1,128)}), f32[16,1,3072]{2,1,0:T(1,128)S(1)}, u32[]{:S(2)}, u32[]{:S(2)}) async-start(f32[16,1,3072]{2,1,0:T(1,128)} %reshape.267), calls=%async_computation | async-start | bytes 393216 | tf_op jit(solution)/shard_map/all_to_all | solution.py:156
  67.5 39.2 %all-to-all-start.1 = ((f32[16,1,3072]{2,1,0:T(1,128)}), f32[16,1,3072]{2,1,0:T(1,128)S(1)}, u32[]{:S(2)}, u32[]{:S(2)}) async-start(f32[16,1,3072]{2,1,0:T(1,128)} %reshape.265), calls=%async_computation.1 | async-start | bytes 393216 | tf_op jit(solution)/shard_map/all_to_all | solution.py:157
  115.0 17.1 %copy-start.2 = (s32[4096,32]{0,1:T(8,128)S(1)}, s32[4096,32]{0,1:T(8,128)}, u32[]{:S(2)}) copy-start(s32[4096,32]{0,1:T(8,128)} %param.20) | copy-start | bytes 1572868
  124.3 16.7 %all-to-all-start.3 = ((f32[64,3,256]{2,1,0:T(4,128)}), f32[64,3,256]{2,1,0:T(4,128)S(1)}, u32[]{:S(2)}, u32[]{:S(2)}) async-start(f32[64,3,256]{2,1,0:T(4,128)} %copy.127), calls=%async_computation.3 | async-start | bytes 524288 | tf_op jit(solution)/shard_map/all_to_all | solution.py:171
  141.0 12.8 %all-to-all-start.4 = ((f32[64,3,256]{2,1,0:T(4,128)}), f32[64,3,256]{2,1,0:T(4,128)S(1)}, u32[]{:S(2)}, u32[]{:S(2)}) async-start(f32[64,3,256]{2,1,0:T(4,128)} %copy.130), calls=%async_computation.4 | async-start | bytes 524288 | tf_op jit(solution)/shard_map/all_to_all | solution.py:172
  144.7 221.8 %all-reduce.2.cloned.1.call-start = ((), (), s32[]{:S(2)}) async-start(), calls=%async_computation.5 | async-start | bytes 786432 | tf_op jit(solution)/shard_map/psum | solution.py:175
  145.0 12.5 %copy-start.1 = (f32[4,3,4096]{2,0,1:T(4,128)}, f32[4,3,4096]{2,0,1:T(4,128)S(1)}, u32[]{:S(2)}) copy-start(f32[4,3,4096]{2,0,1:T(4,128)S(1)} %all_to_all.80) | copy-start | bytes 589828
  145.0 9.4 %collective-permute-start.1 = (f32[4,3,128]{2,0,1:T(4,128)S(1)}, f32[4,3,128]{2,0,1:T(4,128)S(1)}, u32[]{:S(2)}, u32[]{:S(2)}) collective-permute-start(f32[4,3,128]{2,0,1:T(4,128)S(1)} %get-tuple-element.152), channel_id=1, source_target_pairs={{1,0},{2,1},{3,2},{4,3},{5,4},{6,5},{7,6},{8,7},{9,8},{10,9},{11,1... | collective-permute-start | bytes 18440 | tf_op jit(solution)/shard_map/ppermute | solution.py:24
  148.4 9.1 %collective-permute-start = (f32[4,3,128]{2,0,1:T(4,128)S(1)}, f32[4,3,128]{2,0,1:T(4,128)S(1)}, u32[]{:S(2)}, u32[]{:S(2)}) collective-permute-start(f32[4,3,128]{2,0,1:T(4,128)S(1)} %get-tuple-element.151), channel_id=1, source_target_pairs={{0,1},{1,2},{2,3},{3,4},{4,5},{5,6},{6,7},{7,8},{8,9},{9,10},{10,1... | collective-permute-start | bytes 18440 | tf_op jit(solution)/shard_map/ppermute | solution.py:23
  367.2 9.1 %collective-permute-start.2 = (f32[8,3,128]{2,0,1:T(8,128)S(1)}, f32[8,3,128]{2,0,1:T(8,128)S(1)}, u32[]{:S(2)}, u32[]{:S(2)}) collective-permute-start(f32[8,3,128]{2,0,1:T(8,128)S(1)} %get-tuple-element.150), channel_id=1, source_target_pairs={{0,1},{1,2},{2,3},{3,4},{4,5},{5,6},{6,7},{7,8},{8,9},{9,10},{10,1... | collective-permute-start | bytes 36872 | tf_op jit(solution)/shard_map/ppermute | solution.py:23
  367.4 10.0 %collective-permute-start.3 = (f32[8,3,128]{2,0,1:T(8,128)S(1)}, f32[8,3,128]{2,0,1:T(8,128)S(1)}, u32[]{:S(2)}, u32[]{:S(2)}) collective-permute-start(f32[8,3,128]{2,0,1:T(8,128)S(1)} %get-tuple-element.149), channel_id=1, source_target_pairs={{1,0},{2,1},{3,2},{4,3},{5,4},{6,5},{7,6},{8,7},{9,8},{10,9},{11,1... | collective-permute-start | bytes 36872 | tf_op jit(solution)/shard_map/ppermute | solution.py:24
  396.0 5.9 %copy-start.6 = (bf16[240,240]{1,0:T(8,128)(2,1)S(1)}, bf16[240,240]{1,0:T(8,128)(2,1)}, u32[]{:S(2)}) copy-start(bf16[240,240]{1,0:T(8,128)(2,1)} %param.23) | copy-start | bytes 345604
  396.8 5.6 %copy-start.7 = (bf16[240,240]{1,0:T(8,128)(2,1)S(1)}, bf16[240,240]{1,0:T(8,128)(2,1)}, u32[]{:S(2)}) copy-start(bf16[240,240]{1,0:T(8,128)(2,1)} %param.24) | copy-start | bytes 345604
  396.8 5.6 %copy-start.8 = (bf16[240,3]{0,1:T(4,128)(2,1)S(1)}, bf16[240,3]{0,1:T(4,128)(2,1)}, u32[]{:S(2)}) copy-start(bf16[240,3]{0,1:T(4,128)(2,1)} %param.25) | copy-start | bytes 4324
Sparse Core Ops, SparseCore 0:
  154.6 160.6 all-reduce.1
where the time goes:
time: 464 us; the launch traced here: 457 us
  local copies, waits for them, and re-layouts  167 us (36%)
  matrix products  81.2 us (18%)
  other arithmetic  69.4 us (15%)
  blocking collectives  45.6 us (10%)
  starting transfers between devices  45 us (10%)
  loops' own time  21.9 us (5%)
  between operations  14.9 us (3%)
  waiting for transfers between devices  12.5 us (3%)
    dot_general x34, matrix products, one_block(): jnp.dot(window, selector, precision=lax.Precision.HIGHEST, preferred_elem...  70.5 us
    unnamed x33, local copies, waits for them, and re-layouts  64.3 us
    all_gather x1, blocking collectives, body(): lax.all_gather(neural, 'bead', axis=2, tiled=True)  45.6 us
    dynamic_update_slice x34, local copies, waits for them, and re-layouts, banded_take(): pieces = lax.map(one_block, jnp.arange(count // block, dtype=jnp.int32))  33.3 us
    sub x34, other arithmetic, one_block(): rows = lax.dynamic_slice_in_dim(lists, number * block, block, 0) - first  27.3 us
    another operation x2, loops' own time, banded_take(): pieces = lax.map(one_block, jnp.arange(count // block, dtype=jnp.int32))  21.9 us
    dynamic_slice x34, local copies, waits for them, and re-layouts, banded_take(): pieces = lax.map(one_block, jnp.arange(count // block, dtype=jnp.int32))  21.5 us
    reduce_sum x1, other arithmetic, pair_forces(): return PAIR_STRENGTH * jnp.sum(apart * closeness, axis=3)  16.5 us
  transfers between devices with their start and end apart: 10, of which 4 were waited for; matrix products, arithmetic and copies ran while one was open for 56% of the time, Pallas kernels for 0%

commit v1 on v0

--- a/solution.py
+++ b/solution.py
@@ -177,7 +177,9 @@
     spread = ratio * jnp.einsum(
         "cb,cxa->bxa",
         local_contract,
-        lax.all_gather(neural, "bead", axis=2, tiled=True),
+        jnp.concatenate(
+            lax.all_to_all(jnp.stack([neural] * lax.axis_size("bead")), "bead", 0, 0), axis=2
+        ),
         precision=best,
     )
     bead_extended = padded(new_q, ((("slab", "grp"), 2),), EDGE)

time: 464 us -> 434 us (0.935)
  the two profiles are of different devices: /device:TPU:0 before, /device:TPU:2 now
where the time goes in v1:
time: 434 us; the launch traced here: 427 us
  local copies, waits for them, and re-layouts  165 us (38%)
  matrix products  82.1 us (19%)
  other arithmetic  74.4 us (17%)
  starting transfers between devices  56.3 us (13%)
  loops' own time  22.3 us (5%)
  between operations  14.8 us (3%)
  waiting for transfers between devices  11.4 us (3%)
    dot_general x34, matrix products, one_block(): jnp.dot(window, selector, precision=lax.Precision.HIGHEST, preferred_elem...  70.5 us
    unnamed x33, local copies, waits for them, and re-layouts  63.4 us
    dynamic_update_slice x34, local copies, waits for them, and re-layouts, banded_take(): pieces = lax.map(one_block, jnp.arange(count // block, dtype=jnp.int32))  33.2 us
    sub x34, other arithmetic, one_block(): rows = lax.dynamic_slice_in_dim(lists, number * block, block, 0) - first  27.2 us
    another operation x2, loops' own time, banded_take(): pieces = lax.map(one_block, jnp.arange(count // block, dtype=jnp.int32))  22.3 us
    dynamic_slice x34, local copies, waits for them, and re-layouts, banded_take(): pieces = lax.map(one_block, jnp.arange(count // block, dtype=jnp.int32))  20.5 us
    reduce_sum x1, other arithmetic, pair_forces(): return PAIR_STRENGTH * jnp.sum(apart * closeness, axis=3)  17.5 us
    reduce_sum x1, other arithmetic, pair_forces(): closeness = 1.0 / (1.0 + jnp.sum(apart * apart, axis=1, keepdims=True))  14.3 us
  transfers between devices with their start and end apart: 11, of which 4 were waited for; matrix products, arithmetic and copies ran while one was open for 61% of the time, Pallas kernels for 0%

profile of v1, /device:TPU:2, one launch (start us, length us, event | category | flops | bytes accessed | tf_op | source)
XLA Modules:
  0.0 426.7 jit_solution(16472265749140795430)
XLA Ops:
  7.2 6.7 %copy.128 = f32[4,3,4096]{0,1,2:T(4,128)} copy(f32[4,3,4096]{2,0,1:T(4,128)} %param.18) | data formatting | bytes 393216 | tf_op args[3]
  13.9 8.9 %reshape.273 = f32[16,1,3072]{2,1,0:T(1,128)} reshape(f32[4096,3,4]{2,1,0:T(4,128)} %bitcast.123) | data formatting | bytes 393216
  22.9 8.9 %all-to-all-start.2 = ((f32[16,1,3072]{2,1,0:T(1,128)}), f32[16,1,3072]{2,1,0:T(1,128)S(1)}, u32[]{:S(2)}, u32[]{:S(2)}) async-start(f32[16,1,3072]{2,1,0:T(1,128)} %reshape.273), calls=%async_computation.2 | async-start | bytes 393216 | tf_op jit(solution)/shard_map/all_to_all | solution.py:158
  31.9 6.0 %copy.122 = f32[4,3,4096]{0,1,2:T(4,128)} copy(f32[4,3,4096]{2,0,1:T(4,128)S(1)} %copy-done.6) | data formatting | bytes 393216 | tf_op args[0]
  37.9 8.9 %reshape.277 = f32[16,1,3072]{2,1,0:T(1,128)} reshape(f32[4096,3,4]{2,1,0:T(4,128)} %bitcast.124) | data formatting | bytes 393216
  47.1 7.5 %all-to-all-start = ((f32[16,1,3072]{2,1,0:T(1,128)}), f32[16,1,3072]{2,1,0:T(1,128)S(1)}, u32[]{:S(2)}, u32[]{:S(2)}) async-start(f32[16,1,3072]{2,1,0:T(1,128)} %reshape.277), calls=%async_computation | async-start | bytes 393216 | tf_op jit(solution)/shard_map/all_to_all | solution.py:156
  54.6 6.0 %copy.125 = f32[4,3,4096]{0,1,2:T(4,128)} copy(f32[4,3,4096]{2,0,1:T(4,128)S(1)} %multiply_add_fusion.2) | data formatting | bytes 393216 | tf_op jit(solution)/shard_map/add | solution.py:154
  60.6 8.9 %reshape.275 = f32[16,1,3072]{2,1,0:T(1,128)} reshape(f32[4096,3,4]{2,1,0:T(4,128)} %bitcast.119) | data formatting | bytes 393216
  69.7 7.9 %all-to-all-start.1 = ((f32[16,1,3072]{2,1,0:T(1,128)}), f32[16,1,3072]{2,1,0:T(1,128)S(1)}, u32[]{:S(2)}, u32[]{:S(2)}) async-start(f32[16,1,3072]{2,1,0:T(1,128)} %reshape.275), calls=%async_computation.1 | async-start | bytes 393216 | tf_op jit(solution)/shard_map/all_to_all | solution.py:157
  80.1 7.2 %reshape.274 = f32[4096,3,4]{2,1,0:T(4,128)} reshape(f32[16,3072]{1,0:T(8,128)S(1)} %reduce.3) | data formatting | bytes 393216
  87.3 6.5 %copy.129 = f32[4,3,16,256]{3,0,2,1:T(4,128)S(1)} copy(f32[4,3,16,256]{0,1,3,2:T(4,128)} %bitcast.120) | data formatting | bytes 393216 | tf_op jit(solution)/shard_map/all_to_all | solution.py:158
  95.0 7.2 %reshape.278 = f32[4096,3,4]{2,1,0:T(4,128)} reshape(f32[16,3072]{1,0:T(8,128)S(1)} %reduce.4) | data formatting | bytes 393216
  102.2 6.5 %copy.123 = f32[4,3,16,256]{3,0,2,1:T(4,128)S(1)} copy(f32[4,3,16,256]{0,1,3,2:T(4,128)} %bitcast.121) | data formatting | bytes 393216 | tf_op jit(solution)/shard_map/all_to_all | solution.py:156
  109.9 7.2 %reshape.276 = f32[4096,3,4]{2,1,0:T(4,128)} reshape(f32[16,3072]{1,0:T(8,128)S(1)} %reduce.5) | data formatting | bytes 393216
  117.1 6.6 %copy.126 = f32[4,3,16,256]{3,0,2,1:T(4,128)S(1)} copy(f32[4,3,16,256]{0,1,3,2:T(4,128)} %bitcast.122) | data formatting | bytes 393216 | tf_op jit(solution)/shard_map/all_to_all | solution.py:157
  126.4 7.5 %all-to-all-start.3 = ((f32[64,3,256]{2,1,0:T(4,128)}), f32[64,3,256]{2,1,0:T(4,128)S(1)}, u32[]{:S(2)}, u32[]{:S(2)}) async-start(f32[64,3,256]{2,1,0:T(4,128)} %copy.130), calls=%async_computation.3 | async-start | bytes 524288 | tf_op jit(solution)/shard_map/all_to_all | solution.py:171
  138.4 3.1 all-to-all-done.3
  141.5 5.5 %all-to-all-start.4 = ((f32[64,3,256]{2,1,0:T(4,128)}), f32[64,3,256]{2,1,0:T(4,128)S(1)}, u32[]{:S(2)}, u32[]{:S(2)}) async-start(f32[64,3,256]{2,1,0:T(4,128)} %copy.133), calls=%async_computation.4 | async-start | bytes 524288 | tf_op jit(solution)/shard_map/all_to_all | solution.py:172
  147.3 3.1 collective-permute-start.1
  152.0 2.7 all-to-all-done.4
  155.3 4.2 collective-permute-done
  159.6 172.9 %while.22 = (s32[]{:T(128)}, f32[32,4,3,128,32]{4,3,2,1,0:T(8,128)}, s32[32]{0:T(128)S(1)}, f32[12,4352]{1,0:T(8,128)S(1)}, s32[4096,32]{1,0:T(8,128)}, /*index=...) while((s32[]{:T(128)}, f32[32,4,3,128,32]{4,3,2,1,0:T(8,128)}, s32[32]{0:T(128)S(1)}, ...), condition=%wide.region_1.2_spmd.clone, body=%wide.region_0.1_spmd.clone.sunk | while | flops 228069376 | bytes 1679568 | solution.py:95
  161.8 2.0 fusion.127
  167.2 2.0 fusion.127
  172.6 2.0 fusion.127
  178.0 2.0 fusion.127
  183.3 2.0 fusion.127
  188.7 2.0 fusion.127
  194.1 2.0 fusion.127
  199.6 2.0 fusion.127
  205.0 2.0 fusion.127
  210.4 2.0 fusion.127
  221.2 2.0 fusion.127
  259.1 2.0 fusion.127
  275.3 2.0 fusion.127
  286.1 2.0 fusion.127
  296.9 2.0 fusion.127
  332.5 14.3 %multiply_reduce_fusion.1 = f32[4,32,128,32]{3,2,0,1:T(8,128)} fusion(f32[32,4,3,128,32]{4,3,2,1,0:T(8,128)} %get-tuple-element.72, f32[4,3,32,128]{3,1,0,2:T(4,128)S(1)} %copy.138), kind=kLoop, calls=%fused_computation.18 | loop fusion | flops 4194304 | bytes 8585216 | tf_op jit(solution)/shard_map/reduce_sum | solution.py:123
  347.5 8.5 %add_divide_fusion = f32[4,32,128,32]{3,2,0,1:T(8,128)} fusion(f32[4,32,128,32]{3,2,0,1:T(8,128)} %multiply_reduce_fusion.1), kind=kLoop, calls=%fused_computation.20 | loop fusion | flops 1048576 | bytes 4194304 | tf_op jit(solution)/shard_map/div | solution.py:123
  356.0 7.9 %collective-permute-start.3 = (f32[8,3,128]{2,0,1:T(8,128)S(1)}, f32[8,3,128]{2,0,1:T(8,128)S(1)}, u32[]{:S(2)}, u32[]{:S(2)}) collective-permute-start(f32[8,3,128]{2,0,1:T(8,128)S(1)} %get-tuple-element.149), channel_id=1, source_target_pairs={{1,0},{2,1},{3,2},{4,3},{5,4},{6,5},{7,6},{8,7},{9,8},{10,9},{11,1... | collective-permute-start | bytes 36872 | tf_op jit(solution)/shard_map/ppermute | solution.py:24
  366.6 11.8 %while.23 = (s32[]{:T(128)}, f32[2,8,3,128,32]{4,3,2,1,0:T(8,128)}, s32[2]{0:T(128)S(1)}, s32[]{:T(128)}, f32[24,4352]{1,0:T(8,128)}, /*index=5*/s32[256,32]{1,0...) while((s32[]{:T(128)}, f32[2,8,3,128,32]{4,3,2,1,0:T(8,128)}, ...), condition=%wide.region_6.7_spmd.clone, body=%wide.region_5.6_spmd.clone.sunk | while | flops 454561792 | bytes 3264749 | solution.py:95
  367.9 2.8 fusion.129
  373.8 2.8 fusion.129
  378.4 2.5 multiply_reduce_fusion.2
  381.5 2.4 copy.144
  385.1 4.6 %fusion.15 = bf16[2048,240]{0,1:T(8,128)(2,1)S(1)} fusion(bf16[1600,240]{0,1:T(8,128)(2,1)S(1)} %copy-done, bf16[128,1600]{0,1:T(8,128)(2,1)} %param.21, bf16[2048,128]{0,1:T(8,128)(2,1)S(1)} %bitcast.142), kind=kOutput, calls=%fused_computation.28 | convolution fusion | flops 2415493120 | bytes 2684928 | tf_op jit(solution)/shard_map/dot_general | solution.py:111
  392.6 7.9 %all-to-all-start.5 = ((f32[16,8,3,256]{3,1,2,0:T(8,128)}), f32[16,8,3,256]{3,1,2,0:T(8,128)S(1)}, u32[]{:S(2)}, u32[]{:S(2)}) async-start(f32[16,8,3,256]{3,1,2,0:T(8,128)} %stack.2), calls=%async_computation.5 | async-start | bytes 786432 | tf_op jit(solution)/shard_map/all_to_all | solution.py:181
  400.4 17.5 %multiply_reduce_fusion = f32[4,3,32,128]{3,1,0,2:T(4,128)S(1)} fusion(f32[32,4,3,128,32]{4,3,2,1,0:T(8,128)} %get-tuple-element.72, f32[4,32,128,32]{3,2,0,1:T(8,128)} %add_divide_fusion, f32[4,3,32,128]{3,1,0,2:T(4,128)S(1)} %copy.138), kind=kLoop, calls=%fused_computation.17 | loop fusion | flops 4669440 | bytes 8781824 | tf_op jit(solution)/shard_map/reduce_sum | solution.py:124
  (294 shorter events, 150.9 us)
Async XLA Ops:
  7.2 378.0 %copy-start = (bf16[1600,240]{0,1:T(8,128)(2,1)S(1)}, bf16[1600,240]{0,1:T(8,128)(2,1)}, u32[]{:S(2)}) copy-start(bf16[1600,240]{0,1:T(8,128)(2,1)} %param.22) | copy-start | bytes 2304004
  7.2 24.6 %copy-start.4 = (f32[4,3,4096]{2,0,1:T(4,128)S(1)}, f32[4,3,4096]{2,0,1:T(4,128)}, u32[]{:S(2)}) copy-start(f32[4,3,4096]{2,0,1:T(4,128)} %param.16) | copy-start | bytes 589828
  7.2 24.6 %copy-start.5 = (f32[4,3,4096]{2,0,1:T(4,128)S(1)}, f32[4,3,4096]{2,0,1:T(4,128)}, u32[]{:S(2)}) copy-start(f32[4,3,4096]{2,0,1:T(4,128)} %param.17) | copy-start | bytes 589828
  7.2 24.7 %copy-start.6 = (f32[4,3,4096]{2,0,1:T(4,128)S(1)}, f32[4,3,4096]{2,0,1:T(4,128)}, u32[]{:S(2)}) copy-start(f32[4,3,4096]{2,0,1:T(4,128)} %param.15) | copy-start | bytes 589828
  22.9 24.2 %all-to-all-start.2 = ((f32[16,1,3072]{2,1,0:T(1,128)}), f32[16,1,3072]{2,1,0:T(1,128)S(1)}, u32[]{:S(2)}, u32[]{:S(2)}) async-start(f32[16,1,3072]{2,1,0:T(1,128)} %reshape.273), calls=%async_computation.2 | async-start | bytes 393216 | tf_op jit(solution)/shard_map/all_to_all | solution.py:158
  47.1 22.6 %all-to-all-start = ((f32[16,1,3072]{2,1,0:T(1,128)}), f32[16,1,3072]{2,1,0:T(1,128)S(1)}, u32[]{:S(2)}, u32[]{:S(2)}) async-start(f32[16,1,3072]{2,1,0:T(1,128)} %reshape.277), calls=%async_computation | async-start | bytes 393216 | tf_op jit(solution)/shard_map/all_to_all | solution.py:156
  69.7 39.1 %all-to-all-start.1 = ((f32[16,1,3072]{2,1,0:T(1,128)}), f32[16,1,3072]{2,1,0:T(1,128)S(1)}, u32[]{:S(2)}, u32[]{:S(2)}) async-start(f32[16,1,3072]{2,1,0:T(1,128)} %reshape.275), calls=%async_computation.1 | async-start | bytes 393216 | tf_op jit(solution)/shard_map/all_to_all | solution.py:157
  117.1 17.0 %copy-start.2 = (s32[4096,32]{0,1:T(8,128)S(1)}, s32[4096,32]{0,1:T(8,128)}, u32[]{:S(2)}) copy-start(s32[4096,32]{0,1:T(8,128)} %param.20) | copy-start | bytes 1572868
  126.4 15.1 %all-to-all-start.3 = ((f32[64,3,256]{2,1,0:T(4,128)}), f32[64,3,256]{2,1,0:T(4,128)S(1)}, u32[]{:S(2)}, u32[]{:S(2)}) async-start(f32[64,3,256]{2,1,0:T(4,128)} %copy.130), calls=%async_computation.3 | async-start | bytes 524288 | tf_op jit(solution)/shard_map/all_to_all | solution.py:171
  141.5 13.2 %all-to-all-start.4 = ((f32[64,3,256]{2,1,0:T(4,128)}), f32[64,3,256]{2,1,0:T(4,128)S(1)}, u32[]{:S(2)}, u32[]{:S(2)}) async-start(f32[64,3,256]{2,1,0:T(4,128)} %copy.133), calls=%async_computation.4 | async-start | bytes 524288 | tf_op jit(solution)/shard_map/all_to_all | solution.py:172
  147.0 199.7 %all-reduce.2.cloned.1.call-start = ((), (), s32[]{:S(2)}) async-start(), calls=%async_computation.6 | async-start | bytes 786432 | tf_op jit(solution)/shard_map/psum | solution.py:175
  147.3 12.3 %copy-start.1 = (f32[4,3,4096]{2,0,1:T(4,128)}, f32[4,3,4096]{2,0,1:T(4,128)S(1)}, u32[]{:S(2)}) copy-start(f32[4,3,4096]{2,0,1:T(4,128)S(1)} %all_to_all.83) | copy-start | bytes 589828
  147.3 8.0 %collective-permute-start.1 = (f32[4,3,128]{2,0,1:T(4,128)S(1)}, f32[4,3,128]{2,0,1:T(4,128)S(1)}, u32[]{:S(2)}, u32[]{:S(2)}) collective-permute-start(f32[4,3,128]{2,0,1:T(4,128)S(1)} %get-tuple-element.152), channel_id=1, source_target_pairs={{1,0},{2,1},{3,2},{4,3},{5,4},{6,5},{7,6},{8,7},{9,8},{10,9},{11,1... | collective-permute-start | bytes 18440 | tf_op jit(solution)/shard_map/ppermute | solution.py:24
  150.4 9.1 %collective-permute-start = (f32[4,3,128]{2,0,1:T(4,128)S(1)}, f32[4,3,128]{2,0,1:T(4,128)S(1)}, u32[]{:S(2)}, u32[]{:S(2)}) collective-permute-start(f32[4,3,128]{2,0,1:T(4,128)S(1)} %get-tuple-element.151), channel_id=1, source_target_pairs={{0,1},{1,2},{2,3},{3,4},{4,5},{5,6},{6,7},{7,8},{8,9},{9,10},{10,1... | collective-permute-start | bytes 18440 | tf_op jit(solution)/shard_map/ppermute | solution.py:23
  347.5 16.3 %copy-start.3 = (f32[8,3,4096]{2,0,1:T(8,128)S(1)}, f32[8,3,4096]{2,0,1:T(8,128)}, u32[]{:S(2)}) copy-start(f32[8,3,4096]{2,0,1:T(8,128)} %all-reduce.2.cloned.1.call-done) | copy-start | bytes 1179652
  347.5 16.3 %collective-permute-start.2 = (f32[8,3,128]{2,0,1:T(8,128)S(1)}, f32[8,3,128]{2,0,1:T(8,128)S(1)}, u32[]{:S(2)}, u32[]{:S(2)}) collective-permute-start(f32[8,3,128]{2,0,1:T(8,128)S(1)} %get-tuple-element.150), channel_id=1, source_target_pairs={{0,1},{1,2},{2,3},{3,4},{4,5},{5,6},{6,7},{7,8},{8,9},{9,10},{10,1... | collective-permute-start | bytes 36872 | tf_op jit(solution)/shard_map/ppermute | solution.py:23
  356.0 9.3 %collective-permute-start.3 = (f32[8,3,128]{2,0,1:T(8,128)S(1)}, f32[8,3,128]{2,0,1:T(8,128)S(1)}, u32[]{:S(2)}, u32[]{:S(2)}) collective-permute-start(f32[8,3,128]{2,0,1:T(8,128)S(1)} %get-tuple-element.149), channel_id=1, source_target_pairs={{1,0},{2,1},{3,2},{4,3},{5,4},{6,5},{7,6},{8,7},{9,8},{10,9},{11,1... | collective-permute-start | bytes 36872 | tf_op jit(solution)/shard_map/ppermute | solution.py:24
  383.9 5.9 %copy-start.7 = (bf16[240,240]{1,0:T(8,128)(2,1)S(1)}, bf16[240,240]{1,0:T(8,128)(2,1)}, u32[]{:S(2)}) copy-start(bf16[240,240]{1,0:T(8,128)(2,1)} %param.23) | copy-start | bytes 345604
  384.6 5.6 %copy-start.8 = (bf16[240,3]{0,1:T(4,128)(2,1)S(1)}, bf16[240,3]{0,1:T(4,128)(2,1)}, u32[]{:S(2)}) copy-start(bf16[240,3]{0,1:T(4,128)(2,1)} %param.25) | copy-start | bytes 4324
  392.6 25.6 %all-to-all-start.5 = ((f32[16,8,3,256]{3,1,2,0:T(8,128)}), f32[16,8,3,256]{3,1,2,0:T(8,128)S(1)}, u32[]{:S(2)}, u32[]{:S(2)}) async-start(f32[16,8,3,256]{3,1,2,0:T(8,128)} %stack.2), calls=%async_computation.5 | async-start | bytes 786432 | tf_op jit(solution)/shard_map/all_to_all | solution.py:181
Sparse Core Ops, SparseCore 0:
  155.4 156.0 all-reduce.1
